TPU v7x, 32 devices: a whole 2x2x4 slice. The times are simulated.
32 devices in a mesh: shell: 8 (over z, core), patch: 4 (over y, x).
Axes of the slice: x: 2, y: 2, z: 4, core: 2. Of those that a mesh axis runs over, the one named last changes fastest.
Arguments:
- field_j: float32 [2, 256, 128, 128], P(None, 'shell', 'patch'), may hold values from -1 to 1
Outputs:
- beta_field: float32 [256, 128, 128], P('shell', 'patch')
- u_field: float32 [2, 256, 128, 128], P(None, 'shell', 'patch')
- w_field: float32 [256, 128, 128], P('shell', 'patch')
- h_field: float32 [2, 256, 128, 128], P(None, 'shell', 'patch')
All inputs are finite; a program needn't handle non-finite values.
Results may differ from a plain program's by a relative error of at most 0.00002.
Values sent between devices are 32-bit elements; how exact they have to be, the bound alone decides.
A program may use at most 64 MiB of HBM per device.

v0:
```python
import math

import jax
import jax.numpy as jnp
from jax import lax
from jax.sharding import PartitionSpec as P


def shifted(block, axis, distance):
    devices = range(lax.axis_size(axis))
    route = [(i - distance, i) for i in devices if i - distance in devices]
    return lax.ppermute(block, axis, route)


def with_halo(shard, sides, width):
    for axis, dim in sides:
        size, length = (lax.axis_size(axis), shard.shape[dim])
        up = [(i, (i + 1) % size) for i in range(size)]
        down = [(j, i) for i, j in up]
        last = lax.slice_in_dim(shard, length - width, length, axis=dim)
        first = lax.slice_in_dim(shard, 0, width, axis=dim)
        before = lax.ppermute(last, axis, up)
        after = lax.ppermute(first, axis, down)
        shard = jnp.concatenate([before, shard, after], axis=dim)
    return shard


def theta_diff(values):
    zero_col = jnp.zeros(values.shape[:-1] + (1,), values.dtype)
    forward = jnp.concatenate([values[..., 1:], zero_col], axis=-1)
    backward = jnp.concatenate([zero_col, values[..., :-1]], axis=-1)
    return 0.5 * (forward - backward)


def crop(values, margin):
    return values[..., margin : values.shape[-2] - margin, :]


def phi_diff(values):
    return 0.5 * (values[..., 2:, :] - values[..., :-2, :])


def spin_diff(real_part, imag_part, orient):
    return (
        theta_diff(crop(real_part, 1)) - orient * phi_diff(imag_part),
        theta_diff(crop(imag_part, 1)) + orient * phi_diff(real_part),
    )


def earlier_total(gathered):
    shells = gathered.shape[0]
    keep_rows = jnp.arange(shells) < lax.axis_index("shell")
    keep_rows = keep_rows.reshape((shells,) + (1,) * (gathered.ndim - 1))
    return jnp.sum(jnp.where(keep_rows, gathered, 0.0), axis=0)


def cumulate(source, below_sum, radial_step):
    return radial_step * (jnp.cumsum(source, axis=-3) + jnp.expand_dims(below_sum, -3))


def beta_integral(source, radial_step):
    shell_sum = jnp.sum(source, axis=-3)
    gathered = lax.all_gather(shell_sum[None], "shell", axis=0, tiled=True)
    below_sum = earlier_total(gathered)
    return cumulate(source, below_sum, radial_step)


def u_integral(source, radial_step):
    shell_sum = jnp.sum(source, axis=-3)
    gathered = lax.all_gather(shell_sum[None], "shell", axis=0, tiled=True)
    below_sum = earlier_total(gathered)
    return cumulate(source, below_sum, radial_step)


def wh_integral(source_w, source_h, radial_step):
    sum_w = jnp.sum(source_w, axis=-3)
    sum_h = jnp.sum(source_h, axis=-3)
    gathered_w, gathered_h = (
        lax.all_gather(sum_w[None], "shell", axis=0, tiled=True),
        lax.all_gather(sum_h[None], "shell", axis=0, tiled=True),
    )
    below_w = earlier_total(gathered_w)
    below_h = earlier_total(gathered_h)
    return (cumulate(source_w, below_w, radial_step), cumulate(source_h, below_h, radial_step))


def source_beta(radial, eth_a, eth_b):
    return 0.25 * (
        0.5 * (radial[0] * radial[0] + radial[1] * radial[1]) - (eth_a * eth_a + eth_b * eth_b)
    )


def source_u(beta_field, beta_re, beta_im, field_j):
    growth = jnp.exp(2.0 * beta_field)
    field_a = field_j[0]
    field_b = field_j[1]
    source_ua = growth * (beta_re - (field_a * beta_re + field_b * beta_im))
    source_ub = growth * (beta_im - (field_b * beta_re - field_a * beta_im))
    return jnp.stack([source_ua, source_ub])


def local(field_j):
    radii_dev = field_j.shape[1]
    shells = lax.axis_size("shell")
    radial_step = 1.0 / math.sqrt(radii_dev * shells)
    arrived = shifted(field_j[:, :1], "shell", -1)
    outermost = lax.axis_index("shell") == shells - 1
    beyond = jnp.where(outermost, field_j[:, -1:], arrived)
    extended = jnp.concatenate([field_j, beyond], axis=1)
    field_rim = with_halo(field_j, (("patch", 2),), 1)
    radial = extended[:, 1:] - extended[:, :-1]
    eth_a, eth_b = spin_diff(field_rim[0], field_rim[1], 1.0)
    barj_a, barj_b = spin_diff(field_rim[0], field_rim[1], -1.0)
    beta_field = beta_integral(source_beta(radial, eth_a, eth_b), radial_step)
    beta_rim = with_halo(beta_field[None], (("patch", 2),), 1)[0]
    beta_re = theta_diff(beta_field)
    beta_im = phi_diff(beta_rim)
    u_field = u_integral(source_u(beta_field, beta_re, beta_im, field_j), radial_step)
    u_rim = with_halo(u_field, (("patch", 2),), 1)
    ethu_a, ethu_b = spin_diff(u_rim[0], u_rim[1], 1.0)
    baru_a, baru_b = spin_diff(u_rim[0], u_rim[1], -1.0)
    growth = jnp.exp(2.0 * beta_field)
    field_a = field_j[0]
    field_b = field_j[1]
    u_a = u_field[0]
    u_b = u_field[1]
    source_w = growth * baru_a + (field_b * u_a - field_a * u_b)
    source_ha = ethu_a + u_a * barj_a - u_b * barj_b + beta_field * field_a
    source_hb = ethu_b + u_a * barj_b + u_b * barj_a + beta_field * field_b
    w_field, h_field = wh_integral(source_w, jnp.stack([source_ha, source_hb]), radial_step)
    return (beta_field, u_field, w_field, h_field)


def solution(mesh):
    return jax.shard_map(
        local,
        mesh=mesh,
        in_specs=(P(None, "shell", "patch", None),),
        out_specs=(
            P("shell", "patch", None),
            P(None, "shell", "patch", None),
            P("shell", "patch", None),
            P(None, "shell", "patch", None),
        ),
        check_vma=False,
    )
```

profile of v0, /device:TPU:25, one launch (start us, length us, event | category | flops | bytes accessed | tf_op | source)
XLA Modules:
  0.0 88.2 jit_solution(15195173211261060184)
XLA Ops:
  0.6 0.9 slice.153
  1.5 2.6 %collective-permute-start = (f32[2,1,32,128]{3,2,1,0:T(8,128)S(1)}, f32[2,1,32,128]{3,2,1,0:T(8,128)S(1)}, u32[]{:S(2)}, u32[]{:S(2)}) collective-permute-start(f32[2,1,32,128]{3,2,1,0:T(8,128)S(1)} %slice.153), channel_id=1, source_target_pairs={{4,0},{8,4},{12,8},{16,12},{20,16},{24,20},{28,24},{5,1},{9,5},{13... | collective-permute-start | bytes 98312 | tf_op jit(solution)/shard_map/ppermute | solution.py:12
  4.1 1.1 %fusion.38 = (f32[2,32,1,128]{3,2,1,0:T(1,128)S(1)}, f32[2,32,1,128]{3,2,1,0:T(1,128)S(1)}) fusion(f32[2,32,32,128]{3,2,1,0:T(8,128)} %param.1), kind=kLoop, calls=%fused_computation.81 | loop fusion | bytes 131072 | tf_op jit(solution)/shard_map/slice | solution.py:20
  5.2 1.3 %collective-permute-start.1 = (f32[2,32,1,128]{3,2,1,0:T(1,128)S(1)}, f32[2,32,1,128]{3,2,1,0:T(1,128)S(1)}, u32[]{:S(2)}, u32[]{:S(2)}) collective-permute-start(f32[2,32,1,128]{3,2,1,0:T(1,128)S(1)} %get-tuple-element.16), channel_id=1, source_target_pairs={{0,1},{1,2},{2,3},{3,0},{4,5},{5,6},{6,7},{7,4},{8,9},{9,10},{10,1... | collective-permute-start | bytes 98312 | tf_op jit(solution)/shard_map/ppermute | solution.py:22
  6.4 1.2 %collective-permute-start.2 = (f32[2,32,1,128]{3,2,1,0:T(1,128)S(1)}, f32[2,32,1,128]{3,2,1,0:T(1,128)S(1)}, u32[]{:S(2)}, u32[]{:S(2)}) collective-permute-start(f32[2,32,1,128]{3,2,1,0:T(1,128)S(1)} %get-tuple-element.17), channel_id=1, source_target_pairs={{1,0},{2,1},{3,2},{0,3},{5,4},{6,5},{7,6},{4,7},{9,8},{10,9},{11,1... | collective-permute-start | bytes 98312 | tf_op jit(solution)/shard_map/ppermute | solution.py:23
  7.6 0.8 slice_select_fusion
  8.4 1.9 %fusion = f32[2,32,32,128]{3,2,1,0:T(8,128)S(1)} fusion(f32[2,32,32,128]{3,2,1,0:T(8,128)} %param.1, f32[2,1,32,128]{3,2,1,0:T(8,128)S(1)} %slice_select_fusion), kind=kLoop, calls=%fused_computation.3 | loop fusion | flops 524288 | bytes 2129920 | tf_op jit(solution)/shard_map/sub | solution.py:111
  10.2 0.2 pad_maximum_fusion
  10.5 0.4 fusion.41
  11.0 0.6 fusion.35
  11.6 14.4 %all-gather = f32[256,128]{1,0:T(8,128)S(1)} all-gather(f32[32,128]{1,0:T(8,128)S(1)} %get-tuple-element.6), channel_id=2, replica_groups=mesh['shell'=8,'patch'=4] {'shell'}, dimensions={0}, use_global_device_ids=true | all-gather | bytes 147456 | tf_op jit(solution)/shard_map/all_gather | solution.py:63
  26.0 1.9 %fusion.45 = f32[32,32,128]{2,1,0:T(8,128)S(1)} fusion(f32[32,32,128]{2,1,0:T(8,128)S(1)} %get-tuple-element.7), kind=kOutput, calls=%fused_computation.88 | output fusion | flops 4063232 | bytes 1048576 | tf_op jit(solution)/shard_map/jit(cumsum)/reduce_window_sum | solution.py:58
  28.1 2.0 %collective-permute-start.3 = (f32[1,32,1,128]{3,2,1,0:T(1,128)S(1)}, f32[1,32,1,128]{3,2,1,0:T(1,128)S(1)}, u32[]{:S(2)}, u32[]{:S(2)}) collective-permute-start(f32[1,32,1,128]{3,2,1,0:T(1,128)S(1)} %get-tuple-element.26), channel_id=1, source_target_pairs={{0,1},{1,2},{2,3},{3,0},{4,5},{5,6},{6,7},{7,4},{8,9},{9,10},{10,1... | collective-permute-start | bytes 49160 | tf_op jit(solution)/shard_map/ppermute | solution.py:22
  30.1 0.4 collective-permute-start.4
  30.6 0.2 fusion.44
  30.8 0.9 %collective-permute-done.3 = f32[1,32,1,128]{3,2,1,0:T(1,128)S(1)} collective-permute-done((f32[1,32,1,128]{3,2,1,0:T(1,128)S(1)}, f32[1,32,1,128]{3,2,1,0:T(1,128)S(1)}, u32[]{:S(2)}, u32[]{:S(2)}) %collective-permute-start.3) | collective-permute-done | bytes 16416 | tf_op jit(solution)/shard_map/ppermute | solution.py:22
  31.7 1.0 %collective-permute-done.4 = f32[1,32,1,128]{3,2,1,0:T(1,128)S(1)} collective-permute-done((f32[1,32,1,128]{3,2,1,0:T(1,128)S(1)}, f32[1,32,1,128]{3,2,1,0:T(1,128)S(1)}, u32[]{:S(2)}, u32[]{:S(2)}) %collective-permute-start.4) | collective-permute-done | bytes 16416 | tf_op jit(solution)/shard_map/ppermute | solution.py:23
  32.8 0.5 fusion.22
  33.3 15.7 %all-gather.1 = f32[16,32,128]{2,1,0:T(8,128)S(1)} all-gather(f32[2,32,128]{2,1,0:T(8,128)S(1)} %fusion.3), channel_id=3, replica_groups=mesh['shell'=8,'patch'=4] {'shell'}, dimensions={0}, use_global_device_ids=true | all-gather | bytes 294912 | tf_op jit(solution)/shard_map/all_gather | solution.py:70
  49.3 1.5 %collective-permute-start.5 = (f32[2,32,1,128]{3,2,1,0:T(1,128)S(1)}, f32[2,32,1,128]{3,2,1,0:T(1,128)S(1)}, u32[]{:S(2)}, u32[]{:S(2)}) collective-permute-start(f32[2,32,1,128]{3,2,1,0:T(1,128)S(1)} %get-tuple-element.14), channel_id=1, source_target_pairs={{0,1},{1,2},{2,3},{3,0},{4,5},{5,6},{6,7},{7,4},{8,9},{9,10},{10,1... | collective-permute-start | bytes 98312 | tf_op jit(solution)/shard_map/ppermute | solution.py:22
  50.8 1.0 %collective-permute-start.6 = (f32[2,32,1,128]{3,2,1,0:T(1,128)S(1)}, f32[2,32,1,128]{3,2,1,0:T(1,128)S(1)}, u32[]{:S(2)}, u32[]{:S(2)}) collective-permute-start(f32[2,32,1,128]{3,2,1,0:T(1,128)S(1)} %get-tuple-element.15), channel_id=1, source_target_pairs={{1,0},{2,1},{3,2},{0,3},{5,4},{6,5},{7,6},{4,7},{9,8},{10,9},{11,1... | collective-permute-start | bytes 98312 | tf_op jit(solution)/shard_map/ppermute | solution.py:23
  51.7 1.3 %collective-permute-done.5 = f32[2,32,1,128]{3,2,1,0:T(1,128)S(1)} collective-permute-done((f32[2,32,1,128]{3,2,1,0:T(1,128)S(1)}, f32[2,32,1,128]{3,2,1,0:T(1,128)S(1)}, u32[]{:S(2)}, u32[]{:S(2)}) %collective-permute-start.5) | collective-permute-done | bytes 32800 | tf_op jit(solution)/shard_map/ppermute | solution.py:22
  53.0 0.8 collective-permute-done.6
  54.1 0.2 fusion.40
  54.4 0.8 fusion.30
  55.2 0.4 fusion.33
  55.6 0.2 fusion.39
  55.8 15.1 %all-gather.2 = f32[256,128]{1,0:T(8,128)S(1)} all-gather(f32[32,128]{1,0:T(8,128)S(1)} %get-tuple-element.4), channel_id=4, replica_groups=mesh['shell'=8,'patch'=4] {'shell'}, dimensions={0}, use_global_device_ids=true | all-gather | bytes 147456 | tf_op jit(solution)/shard_map/all_gather | solution.py:79
  71.0 0.8 fusion.11
  71.9 14.2 %all-gather.3 = f32[16,32,128]{2,1,0:T(8,128)S(1)} all-gather(f32[2,32,128]{2,1,0:T(8,128)S(1)} %fusion.1), channel_id=5, replica_groups=mesh['shell'=8,'patch'=4] {'shell'}, dimensions={0}, use_global_device_ids=true | all-gather | bytes 294912 | tf_op jit(solution)/shard_map/all_gather | solution.py:80
  86.2 1.1 %add_multiply_fusion = f32[2,32,32,128]{3,2,1,0:T(8,128)} fusion(f32[1,32,32,128]{3,2,1,0:T(8,128)S(1)} %fusion.11, f32[1,32,32,128]{3,2,1,0:T(8,128)S(1)} %fusion.30, f32[2,32,128]{2,1,0:T(8,128)S(1)} %select_reduce_fusion), kind=kOutput, calls=%fused_computation.6 | output fusion | flops 8912896 | bytes 2129920 | tf_op jit(solution)/shard_map/jit(cumsum)/reduce_window_sum | solution.py:58
  87.3 0.9 fusion.5
  (25 shorter events, 1.3 us)
Async XLA Ops:
  0.6 9.6 %copy-start = (f32[2,32,32,128]{3,2,1,0:T(8,128)S(1)}, f32[2,32,32,128]{3,2,1,0:T(8,128)}, u32[]{:S(2)}) copy-start(f32[2,32,32,128]{3,2,1,0:T(8,128)} %param.1) | copy-start | bytes 3145732
  1.5 6.1 %collective-permute-start = (f32[2,1,32,128]{3,2,1,0:T(8,128)S(1)}, f32[2,1,32,128]{3,2,1,0:T(8,128)S(1)}, u32[]{:S(2)}, u32[]{:S(2)}) collective-permute-start(f32[2,1,32,128]{3,2,1,0:T(8,128)S(1)} %slice.153), channel_id=1, source_target_pairs={{4,0},{8,4},{12,8},{16,12},{20,16},{24,20},{28,24},{5,1},{9,5},{13... | collective-permute-start | bytes 98312 | tf_op jit(solution)/shard_map/ppermute | solution.py:12
  5.2 5.1 %collective-permute-start.1 = (f32[2,32,1,128]{3,2,1,0:T(1,128)S(1)}, f32[2,32,1,128]{3,2,1,0:T(1,128)S(1)}, u32[]{:S(2)}, u32[]{:S(2)}) collective-permute-start(f32[2,32,1,128]{3,2,1,0:T(1,128)S(1)} %get-tuple-element.16), channel_id=1, source_target_pairs={{0,1},{1,2},{2,3},{3,0},{4,5},{5,6},{6,7},{7,4},{8,9},{9,10},{10,1... | collective-permute-start | bytes 98312 | tf_op jit(solution)/shard_map/ppermute | solution.py:22
  6.4 3.8 %collective-permute-start.2 = (f32[2,32,1,128]{3,2,1,0:T(1,128)S(1)}, f32[2,32,1,128]{3,2,1,0:T(1,128)S(1)}, u32[]{:S(2)}, u32[]{:S(2)}) collective-permute-start(f32[2,32,1,128]{3,2,1,0:T(1,128)S(1)} %get-tuple-element.17), channel_id=1, source_target_pairs={{1,0},{2,1},{3,2},{0,3},{5,4},{6,5},{7,6},{4,7},{9,8},{10,9},{11,1... | collective-permute-start | bytes 98312 | tf_op jit(solution)/shard_map/ppermute | solution.py:23
  28.1 4.7 %copy-start.2 = (f32[32,32,128]{2,1,0:T(8,128)}, f32[32,32,128]{2,1,0:T(8,128)S(1)}, u32[]{:S(2)}) copy-start(f32[32,32,128]{2,1,0:T(8,128)S(1)} %add_multiply_fusion.2) | copy-start | bytes 1572868
  28.1 3.5 %collective-permute-start.3 = (f32[1,32,1,128]{3,2,1,0:T(1,128)S(1)}, f32[1,32,1,128]{3,2,1,0:T(1,128)S(1)}, u32[]{:S(2)}, u32[]{:S(2)}) collective-permute-start(f32[1,32,1,128]{3,2,1,0:T(1,128)S(1)} %get-tuple-element.26), channel_id=1, source_target_pairs={{0,1},{1,2},{2,3},{3,0},{4,5},{5,6},{6,7},{7,4},{8,9},{9,10},{10,1... | collective-permute-start | bytes 49160 | tf_op jit(solution)/shard_map/ppermute | solution.py:22
  30.1 2.6 %collective-permute-start.4 = (f32[1,32,1,128]{3,2,1,0:T(1,128)S(1)}, f32[1,32,1,128]{3,2,1,0:T(1,128)S(1)}, u32[]{:S(2)}, u32[]{:S(2)}) collective-permute-start(f32[1,32,1,128]{3,2,1,0:T(1,128)S(1)} %get-tuple-element.27), channel_id=1, source_target_pairs={{1,0},{2,1},{3,2},{0,3},{5,4},{6,5},{7,6},{4,7},{9,8},{10,9},{11,1... | collective-permute-start | bytes 49160 | tf_op jit(solution)/shard_map/ppermute | solution.py:23
  49.3 21.8 %copy-start.1 = (f32[2,32,32,128]{3,2,1,0:T(8,128)}, f32[2,32,32,128]{3,2,1,0:T(8,128)S(1)}, u32[]{:S(2)}) copy-start(f32[2,32,32,128]{3,2,1,0:T(8,128)S(1)} %add_multiply_fusion.1) | copy-start | bytes 3145732
  49.3 3.7 %collective-permute-start.5 = (f32[2,32,1,128]{3,2,1,0:T(1,128)S(1)}, f32[2,32,1,128]{3,2,1,0:T(1,128)S(1)}, u32[]{:S(2)}, u32[]{:S(2)}) collective-permute-start(f32[2,32,1,128]{3,2,1,0:T(1,128)S(1)} %get-tuple-element.14), channel_id=1, source_target_pairs={{0,1},{1,2},{2,3},{3,0},{4,5},{5,6},{6,7},{7,4},{8,9},{9,10},{10,1... | collective-permute-start | bytes 98312 | tf_op jit(solution)/shard_map/ppermute | solution.py:22
  50.8 3.1 %collective-permute-start.6 = (f32[2,32,1,128]{3,2,1,0:T(1,128)S(1)}, f32[2,32,1,128]{3,2,1,0:T(1,128)S(1)}, u32[]{:S(2)}, u32[]{:S(2)}) collective-permute-start(f32[2,32,1,128]{3,2,1,0:T(1,128)S(1)} %get-tuple-element.15), channel_id=1, source_target_pairs={{1,0},{2,1},{3,2},{0,3},{5,4},{6,5},{7,6},{4,7},{9,8},{10,9},{11,1... | collective-permute-start | bytes 98312 | tf_op jit(solution)/shard_map/ppermute | solution.py:23
where the time goes:
time: 89.8 us; the launch traced here: 88.2 us
  blocking collectives  59.4 us (66%)
  other arithmetic  10.8 us (12%)
  starting transfers between devices  9.82 us (11%)
  waiting for transfers between devices  4.04 us (4%)
  local copies, waits for them, and re-layouts  3.27 us (4%)
    all_gather x1, blocking collectives, u_integral(): gathered = lax.all_gather(shell_sum[None], 'shell', axis=0, tiled=True)  15.7 us
    all_gather x1, blocking collectives, wh_integral(): lax.all_gather(sum_w[None], 'shell', axis=0, tiled=True)  15.1 us
    all_gather x1, blocking collectives, beta_integral(): gathered = lax.all_gather(shell_sum[None], 'shell', axis=0, tiled=True)  14.4 us
    all_gather x1, blocking collectives, wh_integral(): lax.all_gather(sum_h[None], 'shell', axis=0, tiled=True)  14.2 us
    ppermute x3, starting transfers between devices, with_halo(): before = lax.ppermute(last, axis, up)  4.69 us
    another operation x4, other arithmetic, cumulate(): jnp.cumsum(source, axis=-3) + jnp.expand_dims(below_sum, -3)  4.01 us
    ppermute x1, starting transfers between devices, shifted(): return lax.ppermute(block, axis, route)  2.57 us
    ppermute x3, starting transfers between devices, with_halo(): after = lax.ppermute(first, axis, down)  2.56 us
  transfers between devices with their start and end apart: 7, of which 4 were waited for; matrix products, arithmetic and copies ran while one was open for 4% of the time, Pallas kernels for 0%

commit v1 on v0

v1 whole, which is shorter than its diff:
```python
import functools
import math

import jax
import jax.numpy as jnp
from jax import lax
from jax.experimental import pallas as pl
from jax.experimental.pallas import tpu as pltpu
from jax.sharding import PartitionSpec as P

PAD = 8


def remote(src, dst, send_sem, recv_sem, shell, patch):
    return pltpu.make_async_remote_copy(
        src_ref=src,
        dst_ref=dst,
        send_sem=send_sem,
        recv_sem=recv_sem,
        device_id=(shell, patch),
        device_id_type=pl.DeviceIdType.MESH,
    )


def kernel(shells, patches, step, j_hbm, beta_out, u_out, w_out, h_out,
           jp, jnext, jedge, jhalo, barj, bp, bedge, bhalo, up, uedge, uhalo,
           cw, ch, sum_b, part_b, tot_b, slot_b, sum_u, part_u, tot_u, slot_u,
           sum_h, part_h, tot_h, slot_h,
           load_sem, store_sem, rad_sem, edge_send, edge_recv, part_sem, send_sem, recv_sem):
    radii, cols, lanes = jp.shape[1], jp.shape[2] - 2 * PAD, jp.shape[3]
    chips = shells // 2
    shell, patch = lax.axis_index("shell"), lax.axis_index("patch")
    chip, core = shell // 2, shell % 2
    partner = shell + 1 - 2 * core
    right = lax.rem(patch + 1, patches)
    left = lax.rem(patch + patches - 1, patches)
    inner = slice(PAD, PAD + cols)
    above = slice(PAD + 1, PAD + cols + 1)
    below = slice(PAD - 1, PAD + cols - 1)

    load = pltpu.make_async_copy(j_hbm, jp.at[:, :, pl.ds(PAD, cols), :], load_sem)
    load.start()
    barrier = pltpu.get_barrier_semaphore()
    for d in range(1, shells):
        pl.semaphore_signal(barrier, inc=1, device_id=(lax.rem(shell + d, shells), patch),
                            device_id_type=pl.DeviceIdType.MESH)
    for p in (left, right):
        pl.semaphore_signal(barrier, inc=1, device_id=(shell, p),
                            device_id_type=pl.DeviceIdType.MESH)

    lane = lax.broadcasted_iota(jnp.int32, (cols, lanes), 1)
    mask_f = jnp.where(lane == lanes - 1, 0.0, 0.5).astype(jnp.float32)
    mask_b = jnp.where(lane == 0, 0.0, 0.5).astype(jnp.float32)

    def theta(x):
        return pltpu.roll(x, lanes - 1, 1) * mask_f - pltpu.roll(x, 1, 1) * mask_b

    def halo(edge, got, field):
        to_left = remote(edge.at[0], got.at[1], edge_send.at[field, 0], edge_recv.at[field, 1], shell, left)
        to_right = remote(edge.at[1], got.at[0], edge_send.at[field, 1], edge_recv.at[field, 0], shell, right)
        return to_left, to_right

    def exchange(stage, own, part, tot, slots):
        rows = own.shape[0]
        half = rows // 2
        first = remote(own, part, part_sem.at[stage, 0], part_sem.at[stage, 1], partner, patch)
        first.start()
        first.wait_recv()
        tot[...] = own[...] + part[...]
        mine = pl.ds(pl.multiple_of(core * half, 8), half)
        for d in range(1, chips):
            @pl.when(chip + d < chips)
            def _():
                for e in range(2):
                    remote(tot.at[mine], slots.at[d - 1, mine], send_sem.at[stage, d - 1, e],
                           recv_sem.at[stage, d - 1, core], (chip + d) * 2 + e, patch).start()

        @pl.when(core == 0)
        def _():
            part[...] = jnp.zeros_like(part)

        for d in range(1, chips):
            @pl.when(chip >= d)
            def _():
                for e in range(2):
                    piece = pl.ds(e * half, half)
                    remote(tot.at[piece], slots.at[d - 1, piece], send_sem.at[stage, d - 1, e],
                           recv_sem.at[stage, d - 1, e], (chip - d) * 2 + e, patch).wait_recv()
                part[...] += slots[d - 1]

    def finish(stage, own, part, tot, slots):
        rows = own.shape[0]
        half = rows // 2
        remote(own, part, part_sem.at[stage, 0], part_sem.at[stage, 1], partner, patch).wait_send()
        mine = pl.ds(pl.multiple_of(core * half, 8), half)
        for d in range(1, chips):
            @pl.when(chip + d < chips)
            def _():
                for e in range(2):
                    remote(tot.at[mine], slots.at[d - 1, mine], send_sem.at[stage, d - 1, e],
                           recv_sem.at[stage, d - 1, core], (chip + d) * 2 + e, patch).wait_send()

    load.wait()

    def pack(k, c):
        for f in range(2):
            jedge[0, f, pl.ds(k, 1), :] = jp[f, k, PAD:PAD + 1, :]
            jedge[1, f, pl.ds(k, 1), :] = jp[f, k, PAD + cols - 1:PAD + cols, :]
        return c

    lax.fori_loop(0, radii, pack, 0, unroll=8)
    pl.semaphore_wait(barrier, shells + 1)

    j_left, j_right = halo(jedge, jhalo, 0)
    j_left.start()
    j_right.start()

    @pl.when(shell > 0)
    def _():
        remote(j_hbm.at[:, 0], jnext, rad_sem.at[0], rad_sem.at[1], shell - 1, patch).start()

    @pl.when(shell == shells - 1)
    def _():
        for f in range(2):
            jnext[f] = jp[f, radii - 1, inner]

    @pl.when(shell < shells - 1)
    def _():
        remote(j_hbm.at[:, 0], jnext, rad_sem.at[0], rad_sem.at[1], shell, patch).wait_recv()

    j_left.wait_recv()
    j_right.wait_recv()

    def unpack(k, c):
        for f in range(2):
            jp[f, k, PAD - 1:PAD, :] = jhalo[0, f, pl.ds(k, 1), :]
            jp[f, k, PAD + cols:PAD + cols + 1, :] = jhalo[1, f, pl.ds(k, 1), :]
        return c

    lax.fori_loop(0, radii, unpack, 0, unroll=8)

    def beta_step(k, next_a, next_b, total):
        a, b = jp[0, k, inner], jp[1, k, inner]
        ra, rb = next_a - a, next_b - b
        ta, tb = theta(a), theta(b)
        pa = 0.5 * (jp[0, k, above] - jp[0, k, below])
        pb = 0.5 * (jp[1, k, above] - jp[1, k, below])
        ea, eb = ta - pb, tb + pa
        barj[0, k] = ta + pb
        barj[1, k] = tb - pa
        total = total + 0.25 * (0.5 * (ra * ra + rb * rb) - (ea * ea + eb * eb))
        bp[k, inner] = total
        bedge[0, pl.ds(k, 1), :] = total[:1]
        bedge[1, pl.ds(k, 1), :] = total[cols - 1:]
        return total

    zero = jnp.zeros((cols, lanes), jnp.float32)
    total = lax.fori_loop(
        0, radii - 1, lambda k, t: beta_step(k, jp[0, k + 1, inner], jp[1, k + 1, inner], t), zero)
    sum_b[...] = beta_step(radii - 1, jnext[0], jnext[1], total)

    exchange(0, sum_b, part_b, tot_b, slot_b)
    for e, row in ((0, 0), (1, cols - 1)):
        bedge[e] = step * (bedge[e] + part_b[row:row + 1, :])
    b_left, b_right = halo(bedge, bhalo, 1)
    b_left.start()
    b_right.start()

    def beta_final(k, c):
        bp[k, inner] = step * (bp[k, inner] + part_b[...])
        return c

    lax.fori_loop(0, radii, beta_final, 0)
    beta_store = pltpu.make_async_copy(bp.at[:, pl.ds(PAD, cols), :], beta_out, store_sem.at[0])
    beta_store.start()
    b_left.wait_recv()
    b_right.wait_recv()

    def u_step(k, carry):
        sa, sb = carry
        bp[k, PAD - 1:PAD, :] = bhalo[0, pl.ds(k, 1), :]
        bp[k, PAD + cols:PAD + cols + 1, :] = bhalo[1, pl.ds(k, 1), :]
        beta = bp[k, inner]
        growth = jnp.exp(2.0 * beta)
        br = theta(beta)
        bi = 0.5 * (bp[k, above] - bp[k, below])
        a, b = jp[0, k, inner], jp[1, k, inner]
        sa = sa + growth * (br - (a * br + b * bi))
        sb = sb + growth * (bi - (b * br - a * bi))
        for f, s in ((0, sa), (1, sb)):
            up[f, k, inner] = s
            uedge[0, f, pl.ds(k, 1), :] = s[:1]
            uedge[1, f, pl.ds(k, 1), :] = s[cols - 1:]
        return sa, sb

    sa, sb = lax.fori_loop(0, radii, u_step, (zero, zero))
    sum_u[:cols] = sa
    sum_u[cols:] = sb
    exchange(1, sum_u, part_u, tot_u, slot_u)
    for e, row in ((0, 0), (1, cols - 1)):
        for f in range(2):
            at = f * cols + row
            uedge[e, f] = step * (uedge[e, f] + part_u[at:at + 1, :])
    u_left, u_right = halo(uedge, uhalo, 2)
    u_left.start()
    u_right.start()

    def u_final(k, c):
        for f in range(2):
            up[f, k, inner] = step * (up[f, k, inner] + part_u[f * cols:(f + 1) * cols])
        return c

    lax.fori_loop(0, radii, u_final, 0)
    u_store = pltpu.make_async_copy(up.at[:, :, pl.ds(PAD, cols), :], u_out, store_sem.at[1])
    u_store.start()
    u_left.wait_recv()
    u_right.wait_recv()

    def wh_step(k, carry):
        sw, sa, sb = carry
        for f in range(2):
            up[f, k, PAD - 1:PAD, :] = uhalo[0, f, pl.ds(k, 1), :]
            up[f, k, PAD + cols:PAD + cols + 1, :] = uhalo[1, f, pl.ds(k, 1), :]
        beta = bp[k, inner]
        growth = jnp.exp(2.0 * beta)
        a, b = jp[0, k, inner], jp[1, k, inner]
        ua, ub = up[0, k, inner], up[1, k, inner]
        ta, tb = theta(ua), theta(ub)
        pa = 0.5 * (up[0, k, above] - up[0, k, below])
        pb = 0.5 * (up[1, k, above] - up[1, k, below])
        ja, jb = barj[0, k], barj[1, k]
        sw = sw + (growth * (ta + pb) + (b * ua - a * ub))
        sa = sa + ((ta - pb) + ua * ja - ub * jb + beta * a)
        sb = sb + ((tb + pa) + ua * jb + ub * ja + beta * b)
        cw[k] = sw
        ch[0, k] = sa
        ch[1, k] = sb
        return sw, sa, sb

    sw, sa, sb = lax.fori_loop(0, radii, wh_step, (zero, zero, zero))
    sum_h[:cols] = sw
    sum_h[cols:2 * cols] = sa
    sum_h[2 * cols:] = sb
    exchange(2, sum_h, part_h, tot_h, slot_h)

    def wh_final(k, c):
        cw[k] = step * (cw[k] + part_h[:cols])
        for f in range(2):
            ch[f, k] = step * (ch[f, k] + part_h[(f + 1) * cols:(f + 2) * cols])
        return c

    lax.fori_loop(0, radii, wh_final, 0)
    w_store = pltpu.make_async_copy(cw, w_out, store_sem.at[2])
    h_store = pltpu.make_async_copy(ch, h_out, store_sem.at[3])
    w_store.start()
    h_store.start()
    for copy in (j_left, j_right, b_left, b_right, u_left, u_right):
        copy.wait_send()

    @pl.when(shell > 0)
    def _():
        remote(j_hbm.at[:, 0], jnext, rad_sem.at[0], rad_sem.at[1], shell - 1, patch).wait_send()

    finish(0, sum_b, part_b, tot_b, slot_b)
    finish(1, sum_u, part_u, tot_u, slot_u)
    finish(2, sum_h, part_h, tot_h, slot_h)
    for copy in (beta_store, u_store, w_store, h_store):
        copy.wait()


def solution(mesh):
    shells, patches = mesh.shape["shell"], mesh.shape["patch"]
    chips = shells // 2

    def local(field_j):
        _, radii, cols, lanes = field_j.shape
        step = 1.0 / math.sqrt(radii * shells)
        f32 = jnp.float32
        vm = lambda *s: pltpu.VMEM(s, f32)
        tall = cols + 2 * PAD
        scratch = [
            vm(2, radii, tall, lanes), vm(2, cols, lanes), vm(2, 2, radii, lanes), vm(2, 2, radii, lanes),
            vm(2, radii, cols, lanes),
            vm(radii, tall, lanes), vm(2, radii, lanes), vm(2, radii, lanes),
            vm(2, radii, tall, lanes), vm(2, 2, radii, lanes), vm(2, 2, radii, lanes),
            vm(radii, cols, lanes), vm(2, radii, cols, lanes),
        ]
        for n in (1, 2, 3):
            scratch += [vm(n * cols, lanes)] * 3 + [vm(max(chips - 1, 1), n * cols, lanes)]
        dma = pltpu.SemaphoreType.DMA
        many = max(chips - 1, 1)
        scratch += [dma, dma((4,)), dma((2,)), dma((3, 2)), dma((3, 2)), dma((3, 2)),
                    dma((3, many, 2)), dma((3, many, 2))]
        field = jax.ShapeDtypeStruct((radii, cols, lanes), f32)
        pair = jax.ShapeDtypeStruct((2, radii, cols, lanes), f32)
        anywhere = pl.BlockSpec(memory_space=pl.ANY)
        return pl.pallas_call(
            functools.partial(kernel, shells, patches, step),
            out_shape=(field, pair, field, pair),
            in_specs=[anywhere],
            out_specs=(anywhere,) * 4,
            scratch_shapes=scratch,
            compiler_params=pltpu.CompilerParams(
                collective_id=0, has_side_effects=True, vmem_limit_bytes=24 * 1024 * 1024),
        )(field_j)

    return jax.shard_map(
        local,
        mesh=mesh,
        in_specs=(P(None, "shell", "patch", None),),
        out_specs=(
            P("shell", "patch", None),
            P(None, "shell", "patch", None),
            P("shell", "patch", None),
            P(None, "shell", "patch", None),
        ),
        check_vma=False,
    )
```

time: 89.8 us -> 40.3 us (0.45); the launches traced: 88.2 us -> 40.2 us
  blocking collectives: 59.4 us -> 0 us
  Pallas kernels: 0 us -> 34.8 us
  other arithmetic: 10.8 us -> 0 us
  starting transfers between devices: 9.82 us -> 0 us
  waiting for transfers between devices: 4.04 us -> 0 us
  local copies, waits for them, and re-layouts: 3.27 us -> 4.75 us
    all_gather x4 -> x0, blocking collectives: 59.4 us -> none  [the longest x1 15.7 us: u_integral(): gathered = lax.all_gather(shell_sum[None], 'shell', axis=0, tiled=True)]
    pallas_call x0 -> x1, Pallas kernels: none -> 34.8 us  [local(): pl.pallas_call(functools.partial(kernel, shells, patches, step), out_shap...]
    ppermute x7 -> x0, starting transfers between devices: 9.82 us -> none  [the longest x3 4.69 us: with_halo(): before = lax.ppermute(last, axis, up)]
    another operation x7 -> x0, other arithmetic: 6.05 us -> none  [the longest x4 4.01 us: cumulate(): jnp.cumsum(source, axis=-3) + jnp.expand_dims(below_sum, -3)]
    unnamed x6, local copies, waits for them, and re-layouts: 0.02 us -> 4.75 us
    ppermute x7 -> x0, waiting for transfers between devices: 4.04 us -> none  [the longest x3 2.22 us: with_halo(): before = lax.ppermute(last, axis, up)]
    slice x8 -> x0, local copies, waits for them, and re-layouts: 3.08 us -> none  [the longest x3 1.16 us: with_halo(): last = lax.slice_in_dim(shard, length - width, length, axis=dim)]
    sub x1 -> x0, other arithmetic: 1.86 us -> none  [local(): radial = extended[:, 1:] - extended[:, :-1]]
  transfers between devices with their start and end apart: 7 -> 0, of which waited for: 4 -> 0; matrix products, arithmetic and copies ran while one was open for 4% -> 0% of each run, Pallas kernels for 0% -> 0%
where the time goes in v1:
time: 40.3 us; the launch traced here: 40.2 us
  Pallas kernels  34.8 us (86%)
  local copies, waits for them, and re-layouts  4.75 us (12%)
  between operations  0.65 us (2%)
    pallas_call x1, Pallas kernels, local(): pl.pallas_call(functools.partial(kernel, shells, patches, step), out_shap...  34.8 us
    unnamed x6, local copies, waits for them, and re-layouts  4.75 us

profile of v1, /device:TPU:25, one launch (start us, length us, event | category | flops | bytes accessed | tf_op | source)
XLA Modules:
  0.0 40.2 jit_solution(1556290595146336385)
XLA Ops:
  0.6 0.0 copy-start
  0.6 1.2 %copy-done = f32[2,32,32,128]{3,2,1,0:T(8,128)S(1)} copy-done((f32[2,32,32,128]{3,2,1,0:T(8,128)S(1)}, f32[2,32,32,128]{3,2,1,0:T(8,128)}, u32[]{:S(2)}) %copy-start) | copy-done | bytes 1048600
  1.9 34.8 %shard_map.46 = (f32[32,32,128]{2,1,0:T(8,128)S(1)}, f32[2,32,32,128]{3,2,1,0:T(8,128)S(1)}, f32[32,32,128]{2,1,0:T(8,128)S(1)}, f32[2,32,32,128]{3,2,1,0:T(8,128)S(1)}) custom-call(f32[2,32,32,128]{3,2,1,0:T(8,128)S(1)} %copy-done), custom_call_target="tpu_custom_call" | custom-call | tf_op jit(solution)/shard_map/pallas_call | solution.py:297
  36.7 0.8 %copy.9 = f32[32,32,128]{2,1,0:T(8,128)} copy(f32[32,32,128]{2,1,0:T(8,128)S(1)} %get-tuple-element.8) | data formatting | bytes 1048576
  37.5 1.0 %copy.10 = f32[2,32,32,128]{3,2,1,0:T(8,128)} copy(f32[2,32,32,128]{3,2,1,0:T(8,128)S(1)} %get-tuple-element.9) | data formatting | bytes 2097152
  38.4 0.8 %copy.11 = f32[32,32,128]{2,1,0:T(8,128)} copy(f32[32,32,128]{2,1,0:T(8,128)S(1)} %get-tuple-element.10) | data formatting | bytes 1048576
  39.2 1.0 %copy.12 = f32[2,32,32,128]{3,2,1,0:T(8,128)} copy(f32[2,32,32,128]{3,2,1,0:T(8,128)S(1)} %get-tuple-element.11) | data formatting | bytes 2097152
Async XLA Ops:
  0.6 1.2 %copy-start = (f32[2,32,32,128]{3,2,1,0:T(8,128)S(1)}, f32[2,32,32,128]{3,2,1,0:T(8,128)}, u32[]{:S(2)}) copy-start(f32[2,32,32,128]{3,2,1,0:T(8,128)} %j_hbm.1) | copy-start | bytes 3145732

commit v2 on v1

v2 whole, which is shorter than its diff:
```python
import functools
import math

import jax
import jax.numpy as jnp
from jax import lax
from jax.experimental import pallas as pl
from jax.experimental.pallas import tpu as pltpu
from jax.sharding import PartitionSpec as P

PAD = 8


def remote(src, dst, send_sem, recv_sem, shell, patch):
    return pltpu.make_async_remote_copy(
        src_ref=src,
        dst_ref=dst,
        send_sem=send_sem,
        recv_sem=recv_sem,
        device_id=(shell, patch),
        device_id_type=pl.DeviceIdType.MESH,
    )


def kernel(shells, patches, step, j_hbm, bp, up, cw, ch, below_h,
           jp, jnext, jedge, jhalo, barj, bedge, bhalo, uedge, uhalo,
           below_b, sum_b, part_b, tot_b, slot_b, pre_b,
           below_u, sum_u, part_u, tot_u, slot_u, pre_u,
           sum_h, part_h, tot_h, slot_h, pre_h,
           rim_b, rtot_b, rpart_b, rslot_b, rim_u, rtot_u, rpart_u, rslot_u,
           load_sem, rad_sem, edge_send, edge_recv, part_sem, send_sem, recv_sem, fwd_sem,
           rpart_send, rpart_recv, rim_send, rim_recv):
    radii, cols, lanes = jp.shape[1], jp.shape[2] - 2 * PAD, jp.shape[3]
    chips = shells // 2
    shell, patch = lax.axis_index("shell"), lax.axis_index("patch")
    chip, core = shell // 2, shell % 2
    partner = shell + 1 - 2 * core
    right = lax.rem(patch + 1, patches)
    left = lax.rem(patch + patches - 1, patches)
    inner = slice(PAD, PAD + cols)
    above = slice(PAD + 1, PAD + cols + 1)
    below = slice(PAD - 1, PAD + cols - 1)
    before, after = slice(PAD - 1, PAD), slice(PAD + cols, PAD + cols + 1)

    load = pltpu.make_async_copy(j_hbm, jp.at[:, :, pl.ds(PAD, cols), :], load_sem)
    load.start()
    barrier = pltpu.get_barrier_semaphore()
    for d in range(shells):
        there = lax.rem(shell + d, shells)
        for p in (patch, left, right):
            if d == 0 and p is patch:
                continue
            pl.semaphore_signal(barrier, inc=1, device_id=(there, p),
                                device_id_type=pl.DeviceIdType.MESH)

    lane = lax.broadcasted_iota(jnp.int32, (8, lanes), 1)
    keep_f = jnp.where(lane == lanes - 1, 0.0, 0.5).astype(jnp.float32)
    keep_b = jnp.where(lane == 0, 0.0, 0.5).astype(jnp.float32)

    def theta(x):
        reps = x.shape[0] // 8
        mf = jnp.concatenate([keep_f] * reps, axis=0) if reps > 1 else keep_f
        mb = jnp.concatenate([keep_b] * reps, axis=0) if reps > 1 else keep_b
        return pltpu.roll(x, lanes - 1, 1) * mf - pltpu.roll(x, 1, 1) * mb

    def halo(edge, got, field):
        to_left = remote(edge.at[0], got.at[1], edge_send.at[field, 0], edge_recv.at[field, 1], shell, left)
        to_right = remote(edge.at[1], got.at[0], edge_send.at[field, 1], edge_recv.at[field, 0], shell, right)
        return to_left, to_right

    def pieces(stage, own, part, tot, slots, both):
        half = own.shape[0] // 2
        mine = pl.ds(pl.multiple_of(core * half, 8), half)
        first = remote(own, part, part_sem.at[stage, 0], part_sem.at[stage, 1], partner, patch)
        sends = []
        for d in range(1, chips):
            if both:
                sends.append([
                    remote(tot.at[mine], slots.at[d - 1, mine], send_sem.at[stage, d - 1, e],
                           recv_sem.at[stage, d - 1, core], (chip + d) * 2 + e, patch)
                    for e in range(2)])
            else:
                sends.append([
                    remote(tot.at[mine], slots.at[d - 1, mine], send_sem.at[stage, d - 1, 0],
                           recv_sem.at[stage, d - 1, 0], (chip + d) * 2 + core, patch)])
        return mine, half, first, sends

    def rim_pieces(stage, rim, rtot, rpart, rslot):
        over = left * (1 - core) + right * core
        near = [
            remote(rim.at[0], rpart.at[1], rpart_send.at[stage, 0], rpart_recv.at[stage, 1], partner, left),
            remote(rim.at[1], rpart.at[0], rpart_send.at[stage, 1], rpart_recv.at[stage, 0], partner, right)]
        far = [[
            remote(rtot.at[core], rslot.at[d - 1, 1 - core], rim_send.at[stage, d - 1, e],
                   rim_recv.at[stage, d - 1, 1 - core], (chip + d) * 2 + e, over)
            for e in range(2)] for d in range(1, chips)]
        return near, far

    def exchange(stage, own, part, tot, slots, pre, out, both, rims=None):
        mine, half, first, sends = pieces(stage, own, part, tot, slots, both)
        first.start()
        if rims is not None:
            rim, rtot, rpart, rslot = rims
            fields = rim.shape[1]
            cols_of = own.shape[0] // fields
            for f in range(fields):
                rim[0, f:f + 1] = own[f * cols_of:f * cols_of + 1]
                rim[1, f:f + 1] = own[(f + 1) * cols_of - 1:(f + 1) * cols_of]
            near, far = rim_pieces(stage, rim, rtot, rpart, rslot)

            @pl.when(core == 0)
            def _():
                for copy in near:
                    copy.start()

        first.wait_recv()
        tot[mine] = own[mine] + part[mine]
        if rims is not None:
            for f in range(fields):
                lo, hi = f * cols_of, (f + 1) * cols_of - 1
                rtot[0, f:f + 1] = own[lo:lo + 1] + part[lo:lo + 1]
                rtot[1, f:f + 1] = own[hi:hi + 1] + part[hi:hi + 1]
        for d in range(1, chips):
            @pl.when(chip + d < chips)
            def _():
                for copy in sends[d - 1]:
                    copy.start()
                if rims is not None:
                    for copy in far[d - 1]:
                        copy.start()

        @pl.when(core == 0)
        def _():
            out[...] = jnp.zeros_like(out)

        @pl.when(core == 1)
        def _():
            out[...] = part[...]
            if rims is not None:
                for copy in near:
                    copy.wait_recv()

        if rims is not None:
            @pl.when(core == 0)
            def _():
                rpart[...] = jnp.zeros_like(rpart)

        if both:
            for d in range(1, chips):
                @pl.when(chip >= d)
                def _():
                    for e in range(2):
                        piece = pl.ds(e * half, half)
                        remote(tot.at[piece], slots.at[d - 1, piece], send_sem.at[stage, d - 1, e],
                               recv_sem.at[stage, d - 1, e], shell, patch).wait_recv()
                    out[...] += slots[d - 1]
        else:
            @pl.when(chip > 0)
            def _():
                pre[mine] = jnp.zeros((half, lanes), jnp.float32)

            for d in range(1, chips):
                @pl.when(chip >= d)
                def _():
                    for copy in sends[d - 1]:
                        copy.wait_recv()
                    pre[mine] += slots[d - 1, mine]

            @pl.when(chip > 0)
            def _():
                fwd = remote(pre.at[mine], pre.at[mine], fwd_sem.at[stage, 0], fwd_sem.at[stage, 1],
                             partner, patch)
                fwd.start()
                fwd.wait_recv()
                out[...] += pre[...]

        if rims is not None:
            for d in range(1, chips):
                @pl.when(chip >= d)
                def _():
                    for e in range(2):
                        remote(rtot.at[e], rslot.at[d - 1, e], rim_send.at[stage, d - 1, 0],
                               rim_recv.at[stage, d - 1, e], shell, patch).wait_recv()
                    rpart[...] += rslot[d - 1]

    def finish(stage, own, part, tot, slots, pre, both, rims=None):
        mine, half, first, sends = pieces(stage, own, part, tot, slots, both)
        first.wait_send()
        if rims is not None:
            near, far = rim_pieces(stage, *rims)

            @pl.when(core == 0)
            def _():
                for copy in near:
                    copy.wait_send()

        for d in range(1, chips):
            @pl.when(chip + d < chips)
            def _():
                for copy in sends[d - 1]:
                    copy.wait_send()
                if rims is not None:
                    for copy in far[d - 1]:
                        copy.wait_send()

        if not both:
            @pl.when(chip > 0)
            def _():
                remote(pre.at[mine], pre.at[mine], fwd_sem.at[stage, 0], fwd_sem.at[stage, 1],
                       partner, patch).wait_send()

    load.wait()

    def pack(k, c):
        for f in range(2):
            jedge[0, f, pl.ds(k, 1), :] = jp[f, k, PAD:PAD + 1, :]
            jedge[1, f, pl.ds(k, 1), :] = jp[f, k, PAD + cols - 1:PAD + cols, :]
        return c

    lax.fori_loop(0, radii, pack, 0, unroll=8)
    pl.semaphore_wait(barrier, 3 * shells - 1)

    j_left, j_right = halo(jedge, jhalo, 0)
    j_left.start()
    j_right.start()

    @pl.when(shell > 0)
    def _():
        remote(j_hbm.at[:, 0], jnext, rad_sem.at[0], rad_sem.at[1], shell - 1, patch).start()

    def beta_step(k, next_of, spans, totals):
        new = []
        for (lo, n), total in zip(spans, totals):
            at = slice(PAD + lo, PAD + lo + n)
            up1 = slice(PAD + lo + 1, PAD + lo + n + 1)
            dn1 = slice(PAD + lo - 1, PAD + lo + n - 1)
            a, b = jp[0, k, at], jp[1, k, at]
            ra, rb = next_of(0, k, lo, n) - a, next_of(1, k, lo, n) - b
            ta, tb = theta(a), theta(b)
            pa = 0.5 * (jp[0, k, up1] - jp[0, k, dn1])
            pb = 0.5 * (jp[1, k, up1] - jp[1, k, dn1])
            ea, eb = ta - pb, tb + pa
            barj[0, k, lo:lo + n] = ta + pb
            barj[1, k, lo:lo + n] = tb - pa
            total = total + 0.25 * (0.5 * (ra * ra + rb * rb) - (ea * ea + eb * eb))
            bp[k, at] = total
            if lo == 0:
                bedge[0, pl.ds(k, 1), :] = total[:1]
            if lo + n == cols:
                bedge[1, pl.ds(k, 1), :] = total[n - 1:]
            new.append(total)
        return tuple(new)

    def from_jp(f, k, lo, n):
        return jp[f, k + 1, PAD + lo:PAD + lo + n]

    def from_next(f, k, lo, n):
        return jnext[f, lo:lo + n]

    def beta_span(spans, middle):
        zeros = tuple(jnp.zeros((n, lanes), jnp.float32) for _, n in spans)
        totals = lax.fori_loop(0, radii - 1, lambda k, t: beta_step(k, from_jp, spans, t), zeros, unroll=2)
        middle()
        totals = beta_step(radii - 1, from_next, spans, totals)
        for (lo, n), total in zip(spans, totals):
            sum_b[lo:lo + n] = total

    def wait_next():
        @pl.when(shell == shells - 1)
        def _():
            for f in range(2):
                jnext[f] = jp[f, radii - 1, inner]

        @pl.when(shell < shells - 1)
        def _():
            remote(j_hbm.at[:, 0], jnext, rad_sem.at[0], rad_sem.at[1], shell, patch).wait_recv()

    beta_span(((8, cols - 16),), wait_next)
    j_left.wait_recv()
    j_right.wait_recv()

    def unpack(k, c):
        for f in range(2):
            jp[f, k, before, :] = jhalo[0, f, pl.ds(k, 1), :]
            jp[f, k, after, :] = jhalo[1, f, pl.ds(k, 1), :]
        return c

    lax.fori_loop(0, radii, unpack, 0, unroll=8)
    beta_span(((0, 8), (cols - 8, 8)), lambda: None)

    b_left, b_right = halo(bedge, bhalo, 1)
    b_left.start()
    b_right.start()
    rims_b = (rim_b, rtot_b, rpart_b, rslot_b)
    exchange(0, sum_b, part_b, tot_b, slot_b, pre_b, below_b, True, rims_b)
    b_left.wait_recv()
    b_right.wait_recv()

    def beta_final(k, c):
        bp[k, inner] = step * (bp[k, inner] + below_b[...])
        bp[k, before] = step * (bhalo[0, pl.ds(k, 1), :] + rpart_b[0])
        bp[k, after] = step * (bhalo[1, pl.ds(k, 1), :] + rpart_b[1])
        return c

    lax.fori_loop(0, radii, beta_final, 0, unroll=2)
    zero = jnp.zeros((cols, lanes), jnp.float32)

    def u_step(k, carry):
        sa, sb = carry
        beta = bp[k, inner]
        growth = jnp.exp(2.0 * beta)
        br = theta(beta)
        bi = 0.5 * (bp[k, above] - bp[k, below])
        a, b = jp[0, k, inner], jp[1, k, inner]
        sa = sa + growth * (br - (a * br + b * bi))
        sb = sb + growth * (bi - (b * br - a * bi))
        for f, s in ((0, sa), (1, sb)):
            up[f, k, inner] = s
            uedge[0, f, pl.ds(k, 1), :] = s[:1]
            uedge[1, f, pl.ds(k, 1), :] = s[cols - 1:]
        return sa, sb

    sa, sb = lax.fori_loop(0, radii, u_step, (zero, zero), unroll=2)
    sum_u[:cols] = sa
    sum_u[cols:] = sb
    u_left, u_right = halo(uedge, uhalo, 2)
    u_left.start()
    u_right.start()
    rims_u = (rim_u, rtot_u, rpart_u, rslot_u)
    exchange(1, sum_u, part_u, tot_u, slot_u, pre_u, below_u, False, rims_u)
    u_left.wait_recv()
    u_right.wait_recv()

    def u_final(k, c):
        for f in range(2):
            up[f, k, inner] = step * (up[f, k, inner] + below_u[f * cols:(f + 1) * cols])
            up[f, k, before] = step * (uhalo[0, f, pl.ds(k, 1), :] + rpart_u[0, f:f + 1])
            up[f, k, after] = step * (uhalo[1, f, pl.ds(k, 1), :] + rpart_u[1, f:f + 1])
        return c

    lax.fori_loop(0, radii, u_final, 0, unroll=2)

    def wh_step(k, carry):
        sw, sa, sb = carry
        beta = bp[k, inner]
        growth = jnp.exp(2.0 * beta)
        a, b = jp[0, k, inner], jp[1, k, inner]
        ua, ub = up[0, k, inner], up[1, k, inner]
        ta, tb = theta(ua), theta(ub)
        pa = 0.5 * (up[0, k, above] - up[0, k, below])
        pb = 0.5 * (up[1, k, above] - up[1, k, below])
        ja, jb = barj[0, k], barj[1, k]
        sw = sw + (growth * (ta + pb) + (b * ua - a * ub))
        sa = sa + ((ta - pb) + ua * ja - ub * jb + beta * a)
        sb = sb + ((tb + pa) + ua * jb + ub * ja + beta * b)
        cw[k] = sw
        ch[0, k] = sa
        ch[1, k] = sb
        return sw, sa, sb

    sw, sa, sb = lax.fori_loop(0, radii, wh_step, (zero, zero, zero), unroll=2)
    sum_h[:cols] = sw
    sum_h[cols:2 * cols] = sa
    sum_h[2 * cols:] = sb
    exchange(2, sum_h, part_h, tot_h, slot_h, pre_h, below_h, False)

    for copy in (j_left, j_right, b_left, b_right, u_left, u_right):
        copy.wait_send()

    @pl.when(shell > 0)
    def _():
        remote(j_hbm.at[:, 0], jnext, rad_sem.at[0], rad_sem.at[1], shell - 1, patch).wait_send()

    finish(0, sum_b, part_b, tot_b, slot_b, pre_b, True, rims_b)
    finish(1, sum_u, part_u, tot_u, slot_u, pre_u, False, rims_u)
    finish(2, sum_h, part_h, tot_h, slot_h, pre_h, False)


def tail(step, bp, up, cw, ch, below_h, beta_out, u_out, w_out, h_out, wv, hv, sems):
    radii, cols = cw.shape[0], cw.shape[1]
    rows = pl.ds(PAD, cols)
    copies = [pltpu.make_async_copy(bp.at[:, rows, :], beta_out, sems.at[0, 0])]
    copies += [pltpu.make_async_copy(up.at[f, :, rows, :], u_out.at[f], sems.at[1, f]) for f in range(2)]
    for copy in copies:
        copy.start()
    parts = 2
    size = radii // parts
    for i in range(parts):
        def wh_final(k, c):
            wv[k] = step * (cw[k] + below_h[:cols])
            for f in range(2):
                hv[f, k] = step * (ch[f, k] + below_h[(f + 1) * cols:(f + 2) * cols])
            return c

        lax.fori_loop(i * size, (i + 1) * size, wh_final, 0, unroll=4)
        at = pl.ds(i * size, size)
        more = [pltpu.make_async_copy(wv.at[at], w_out.at[at], sems.at[2, i]),
                pltpu.make_async_copy(hv.at[:, at], h_out.at[:, at], sems.at[3, i])]
        for copy in more:
            copy.start()
        copies += more
    for copy in copies:
        copy.wait()


def solution(mesh):
    shells, patches = mesh.shape["shell"], mesh.shape["patch"]
    chips = shells // 2

    def local(field_j):
        _, radii, cols, lanes = field_j.shape
        step = 1.0 / math.sqrt(radii * shells)
        f32 = jnp.float32
        vm = lambda *s: pltpu.VMEM(s, f32)
        tall = cols + 2 * PAD
        scratch = [
            vm(2, radii, tall, lanes), vm(2, cols, lanes), vm(2, 2, radii, lanes), vm(2, 2, radii, lanes),
            vm(2, radii, cols, lanes),
            vm(2, radii, lanes), vm(2, radii, lanes),
            vm(2, 2, radii, lanes), vm(2, 2, radii, lanes),
        ]
        many = max(chips - 1, 1)
        for n in (1, 2, 3):
            if n < 3:
                scratch.append(vm(n * cols, lanes))
            scratch += [vm(n * cols, lanes)] * 3 + [vm(many, n * cols, lanes), vm(n * cols, lanes)]
        for n in (1, 2):
            scratch += [vm(2, n, lanes)] * 3 + [vm(many, 2, n, lanes)]
        dma = pltpu.SemaphoreType.DMA
        scratch += [dma, dma((2,)), dma((3, 2)), dma((3, 2)), dma((3, 2)),
                    dma((3, many, 2)), dma((3, many, 2)), dma((3, 2)),
                    dma((2, 2)), dma((2, 2)), dma((2, many, 2)), dma((2, many, 2))]
        shape = lambda *s: jax.ShapeDtypeStruct(s, f32)
        vmem = pl.BlockSpec(memory_space=pltpu.VMEM)
        hbm = pl.BlockSpec(memory_space=pltpu.HBM)
        found = pl.pallas_call(
            functools.partial(kernel, shells, patches, step),
            out_shape=(shape(radii, tall, lanes), shape(2, radii, tall, lanes), shape(radii, cols, lanes),
                       shape(2, radii, cols, lanes), shape(3 * cols, lanes)),
            in_specs=[hbm],
            out_specs=(vmem,) * 5,
            scratch_shapes=scratch,
            compiler_params=pltpu.CompilerParams(
                collective_id=0, has_side_effects=True, vmem_limit_bytes=24 * 1024 * 1024),
        )(field_j)
        return pl.pallas_call(
            functools.partial(tail, step),
            out_shape=(shape(radii, cols, lanes), shape(2, radii, cols, lanes), shape(radii, cols, lanes),
                       shape(2, radii, cols, lanes)),
            in_specs=[vmem] * 5,
            out_specs=(hbm,) * 4,
            scratch_shapes=[vm(radii, cols, lanes), vm(2, radii, cols, lanes), dma((4, 2))],
            compiler_params=pltpu.CompilerParams(vmem_limit_bytes=24 * 1024 * 1024),
        )(*found)

    return jax.shard_map(
        local,
        mesh=mesh,
        in_specs=(P(None, "shell", "patch", None),),
        out_specs=(
            P("shell", "patch", None),
            P(None, "shell", "patch", None),
            P("shell", "patch", None),
            P(None, "shell", "patch", None),
        ),
        check_vma=False,
    )
```

time: 40.3 us -> 32.2 us (0.80)
  Pallas kernels: 34.8 us -> 30.2 us
  local copies, waits for them, and re-layouts: 4.75 us -> 1.22 us
    pallas_call x1, Pallas kernels: 34.8 us -> 28.4 us  [local(): pl.pallas_call(functools.partial(kernel, shells, patches, step), out_shap...]
    unnamed x6 -> x2, local copies, waits for them, and re-layouts: 4.75 us -> 1.22 us
    pallas_call x0 -> x1, Pallas kernels: none -> 1.73 us  [local(): pl.pallas_call(functools.partial(tail, step), out_shape=(shape(radii, col...]
where the time goes in v2:
time: 32.2 us; the launch traced here: 32 us
  Pallas kernels  30.2 us (94%)
  local copies, waits for them, and re-layouts  1.22 us (4%)
  between operations  0.65 us (2%)
    pallas_call x1, Pallas kernels, local(): pl.pallas_call(functools.partial(kernel, shells, patches, step), out_shap...  28.4 us
    pallas_call x1, Pallas kernels, local(): pl.pallas_call(functools.partial(tail, step), out_shape=(shape(radii, col...  1.73 us
    unnamed x2, local copies, waits for them, and re-layouts  1.22 us

profile of v2, /device:TPU:25, one launch (start us, length us, event | category | flops | bytes accessed | tf_op | source)
XLA Modules:
  0.0 32.0 jit_solution(16720872003314330198)
XLA Ops:
  0.6 0.0 copy-start
  0.6 1.2 %copy-done = f32[2,32,32,128]{3,2,1,0:T(8,128)S(1)} copy-done((f32[2,32,32,128]{3,2,1,0:T(8,128)S(1)}, f32[2,32,32,128]{3,2,1,0:T(8,128)}, u32[]{:S(2)}) %copy-start) | copy-done | bytes 1048600
  1.9 28.4 %shard_map.46 = (f32[32,48,128]{2,1,0:T(8,128)S(1)}, f32[2,32,48,128]{3,2,1,0:T(8,128)S(1)}, f32[32,32,128]{2,1,0:T(8,128)S(1)}, f32[2,32,32,128]{3,2,1,0:T(8,128)S(1)}, f32[96,128]{1,0:T(8,128)S(1)}) custom-call(f32[2,32,32,128]{3,2,1,0:T(8,128)S(1)} %copy-done), custom_call_target="tpu_custom_call" | custom-call | tf_op jit(solution)/shard_map/pallas_call | solution.py:436
  30.3 1.7 %shard_map.47 = (f32[32,32,128]{2,1,0:T(8,128)}, f32[2,32,32,128]{3,2,1,0:T(8,128)}, f32[32,32,128]{2,1,0:T(8,128)}, f32[2,32,32,128]{3,2,1,0:T(8,128)}) custom-call(f32[32,48,128]{2,1,0:T(8,128)S(1)} %get-tuple-element.9.bp, f32[2,32,48,128]{3,2,1,0:T(8,128)S(1)} %get-tuple-element.10.up, f32[32,32,128]{2,1,0:T(8,128)S(1)} %get-tuple-element.11.cw, ...), custom_call_target="tpu_custom_call" | custom-call | tf_op jit(solution)/shard_map/pallas_call | solution.py:446
Async XLA Ops:
  0.6 1.2 %copy-start = (f32[2,32,32,128]{3,2,1,0:T(8,128)S(1)}, f32[2,32,32,128]{3,2,1,0:T(8,128)}, u32[]{:S(2)}) copy-start(f32[2,32,32,128]{3,2,1,0:T(8,128)} %j_hbm.1) | copy-start | bytes 3145732

commit v3 on v2

--- a/solution.py
+++ b/solution.py
@@ -9,6 +9,7 @@
 from jax.sharding import PartitionSpec as P
 
 PAD = 8
+KERNEL_VMEM = 24 * 1024 * 1024
 
 
 def remote(src, dst, send_sem, recv_sem, shell, patch):
@@ -22,11 +23,12 @@
     )
 
 
-def kernel(shells, patches, step, j_hbm, bp, up, cw, ch, below_h,
+def kernel(shells, patches, step, j_hbm, bp, up, cw, ch,
            jp, jnext, jedge, jhalo, barj, bedge, bhalo, uedge, uhalo,
+           es, ej, gs, moment, offb, gain, slope, offu, lift,
            below_b, sum_b, part_b, tot_b, slot_b, pre_b,
            below_u, sum_u, part_u, tot_u, slot_u, pre_u,
-           sum_h, part_h, tot_h, slot_h, pre_h,
+           below_h, sum_h, part_h, tot_h, slot_h, pre_h,
            rim_b, rtot_b, rpart_b, rslot_b, rim_u, rtot_u, rpart_u, rslot_u,
            load_sem, rad_sem, edge_send, edge_recv, part_sem, send_sem, recv_sem, fwd_sem,
            rpart_send, rpart_recv, rim_send, rim_recv):
@@ -96,7 +98,7 @@
             for e in range(2)] for d in range(1, chips)]
         return near, far
 
-    def exchange(stage, own, part, tot, slots, pre, out, both, rims=None):
+    def exchange(stage, own, part, tot, slots, pre, out, both, rims=None, between=None):
         mine, half, first, sends = pieces(stage, own, part, tot, slots, both)
         first.start()
         if rims is not None:
@@ -128,6 +130,9 @@
                 if rims is not None:
                     for copy in far[d - 1]:
                         copy.start()
+
+        if between is not None:
+            between()
 
         @pl.when(core == 0)
         def _():
@@ -292,77 +297,151 @@
     b_left.start()
     b_right.start()
     rims_b = (rim_b, rtot_b, rpart_b, rslot_b)
-    exchange(0, sum_b, part_b, tot_b, slot_b, pre_b, below_b, True, rims_b)
-    b_left.wait_recv()
-    b_right.wait_recv()
-
-    def beta_final(k, c):
-        bp[k, inner] = step * (bp[k, inner] + below_b[...])
-        bp[k, before] = step * (bhalo[0, pl.ds(k, 1), :] + rpart_b[0])
-        bp[k, after] = step * (bhalo[1, pl.ds(k, 1), :] + rpart_b[1])
-        return c
-
-    lax.fori_loop(0, radii, beta_final, 0, unroll=2)
     zero = jnp.zeros((cols, lanes), jnp.float32)
 
-    def u_step(k, carry):
-        sa, sb = carry
-        beta = bp[k, inner]
-        growth = jnp.exp(2.0 * beta)
-        br = theta(beta)
-        bi = 0.5 * (bp[k, above] - bp[k, below])
-        a, b = jp[0, k, inner], jp[1, k, inner]
-        sa = sa + growth * (br - (a * br + b * bi))
-        sb = sb + growth * (bi - (b * br - a * bi))
-        for f, s in ((0, sa), (1, sb)):
-            up[f, k, inner] = s
-            uedge[0, f, pl.ds(k, 1), :] = s[:1]
-            uedge[1, f, pl.ds(k, 1), :] = s[cols - 1:]
-        return sa, sb
-
-    sa, sb = lax.fori_loop(0, radii, u_step, (zero, zero), unroll=2)
+    def u_local():
+        def gather(k, carry):
+            ma, mb, na, nb = carry
+            return (ma + jp[0, k, inner], mb + jp[1, k, inner], na + barj[0, k], nb + barj[1, k])
+
+        for f, m in enumerate(lax.fori_loop(0, radii, gather, (zero,) * 4, unroll=2)):
+            moment[f] = m
+        b_left.wait_recv()
+        b_right.wait_recv()
+
+        def rim_in(k, c):
+            bp[k, before] = bhalo[0, pl.ds(k, 1), :]
+            bp[k, after] = bhalo[1, pl.ds(k, 1), :]
+            return c
+
+        lax.fori_loop(0, radii, rim_in, 0, unroll=8)
+
+        def u_step(k, carry):
+            sa, sb, se, sea, seb = carry
+            raw = bp[k, inner]
+            grow = jnp.exp((2.0 * step) * raw)
+            gs[k] = grow
+            br = step * theta(raw)
+            bi = (0.5 * step) * (bp[k, above] - bp[k, below])
+            a, b = jp[0, k, inner], jp[1, k, inner]
+            sa = sa + grow * (br - (a * br + b * bi))
+            sb = sb + grow * (bi - (b * br - a * bi))
+            se, sea, seb = se + grow, sea + grow * a, seb + grow * b
+            up[0, k, inner] = sa
+            up[1, k, inner] = sb
+            es[k] = se
+            ej[0, k] = sea
+            ej[1, k] = seb
+            return sa, sb, se, sea, seb
+
+        lax.fori_loop(0, radii, u_step, (zero,) * 5)
+
+    exchange(0, sum_b, part_b, tot_b, slot_b, pre_b, below_b, True, rims_b, u_local)
+    offb[inner] = step * below_b[...]
+    offb[before] = step * rpart_b[0]
+    offb[after] = step * rpart_b[1]
+    gain[...] = jnp.exp(2.0 * offb[inner])
+    slope[0] = theta(offb[inner])
+    slope[1] = 0.5 * (offb[above] - offb[below])
+
+    def u_sums(k):
+        dr, di = slope[0], slope[1]
+        e, ea, eb = es[k], ej[0, k], ej[1, k]
+        return (gain[...] * (up[0, k, inner] + (e - ea) * dr - eb * di),
+                gain[...] * (up[1, k, inner] + (e + ea) * di - eb * dr))
+
+    sa, sb = u_sums(radii - 1)
     sum_u[:cols] = sa
     sum_u[cols:] = sb
     u_left, u_right = halo(uedge, uhalo, 2)
-    u_left.start()
-    u_right.start()
+
+    def wh_local():
+        def u_apply(k, c):
+            for f, s in enumerate(u_sums(k)):
+                s = step * s
+                up[f, k, inner] = s
+                uedge[0, f, pl.ds(k, 1), :] = s[:1]
+                uedge[1, f, pl.ds(k, 1), :] = s[cols - 1:]
+            return c
+
+        lax.fori_loop(0, radii, u_apply, 0, unroll=2)
+        u_left.start()
+        u_right.start()
+
+        def b_apply(k, c):
+            bp[k, inner] = step * bp[k, inner] + offb[inner]
+            gs[k] = gain[...] * gs[k]
+            return c
+
+        lax.fori_loop(0, radii, b_apply, 0, unroll=2)
+        u_left.wait_recv()
+        u_right.wait_recv()
+
+        def rim_in(k, c):
+            for f in range(2):
+                up[f, k, before] = uhalo[0, f, pl.ds(k, 1), :]
+                up[f, k, after] = uhalo[1, f, pl.ds(k, 1), :]
+            return c
+
+        lax.fori_loop(0, radii, rim_in, 0, unroll=8)
+
+        def wh_step(k, carry):
+            sw, sa, sb = carry
+            beta = bp[k, inner]
+            a, b = jp[0, k, inner], jp[1, k, inner]
+            ua, ub = up[0, k, inner], up[1, k, inner]
+            ta, tb = theta(ua), theta(ub)
+            pa = 0.5 * (up[0, k, above] - up[0, k, below])
+            pb = 0.5 * (up[1, k, above] - up[1, k, below])
+            ja, jb = barj[0, k], barj[1, k]
+            sw = sw + (gs[k] * (ta + pb) + (b * ua - a * ub))
+            sa = sa + ((ta - pb) + ua * ja - ub * jb + beta * a)
+            sb = sb + ((tb + pa) + ua * jb + ub * ja + beta * b)
+            cw[k] = sw
+            ch[0, k] = sa
+            ch[1, k] = sb
+            return sw, sa, sb
+
+        lax.fori_loop(0, radii, wh_step, (zero,) * 3)
+
     rims_u = (rim_u, rtot_u, rpart_u, rslot_u)
-    exchange(1, sum_u, part_u, tot_u, slot_u, pre_u, below_u, False, rims_u)
-    u_left.wait_recv()
-    u_right.wait_recv()
-
-    def u_final(k, c):
-        for f in range(2):
-            up[f, k, inner] = step * (up[f, k, inner] + below_u[f * cols:(f + 1) * cols])
-            up[f, k, before] = step * (uhalo[0, f, pl.ds(k, 1), :] + rpart_u[0, f:f + 1])
-            up[f, k, after] = step * (uhalo[1, f, pl.ds(k, 1), :] + rpart_u[1, f:f + 1])
-        return c
-
-    lax.fori_loop(0, radii, u_final, 0, unroll=2)
-
-    def wh_step(k, carry):
-        sw, sa, sb = carry
-        beta = bp[k, inner]
-        growth = jnp.exp(2.0 * beta)
-        a, b = jp[0, k, inner], jp[1, k, inner]
-        ua, ub = up[0, k, inner], up[1, k, inner]
-        ta, tb = theta(ua), theta(ub)
-        pa = 0.5 * (up[0, k, above] - up[0, k, below])
-        pb = 0.5 * (up[1, k, above] - up[1, k, below])
-        ja, jb = barj[0, k], barj[1, k]
-        sw = sw + (growth * (ta + pb) + (b * ua - a * ub))
-        sa = sa + ((ta - pb) + ua * ja - ub * jb + beta * a)
-        sb = sb + ((tb + pa) + ua * jb + ub * ja + beta * b)
-        cw[k] = sw
-        ch[0, k] = sa
-        ch[1, k] = sb
-        return sw, sa, sb
-
-    sw, sa, sb = lax.fori_loop(0, radii, wh_step, (zero, zero, zero), unroll=2)
-    sum_h[:cols] = sw
-    sum_h[cols:2 * cols] = sa
-    sum_h[2 * cols:] = sb
-    exchange(2, sum_h, part_h, tot_h, slot_h, pre_h, below_h, False)
+    exchange(1, sum_u, part_u, tot_u, slot_u, pre_u, below_u, False, rims_u, wh_local)
+    for f in range(2):
+        offu[f, inner] = step * below_u[f * cols:(f + 1) * cols]
+        offu[f, before] = step * rpart_u[0, f:f + 1]
+        offu[f, after] = step * rpart_u[1, f:f + 1]
+    oa, ob = offu[0, inner], offu[1, inner]
+    ta, tb = theta(oa), theta(ob)
+    pa = 0.5 * (offu[0, above] - offu[0, below])
+    pb = 0.5 * (offu[1, above] - offu[1, below])
+    lift[0], lift[1], lift[2] = ta + pb, ta - pb, tb + pa
+    ma, mb, na, nb = moment[0], moment[1], moment[2], moment[3]
+    top = radii - 1
+    sum_h[:cols] = cw[top] + (gain[...] * es[top]) * lift[0] + (mb * oa - ma * ob)
+    sum_h[cols:2 * cols] = ch[0, top] + float(radii) * lift[1] + (na * oa - nb * ob)
+    sum_h[2 * cols:] = ch[1, top] + float(radii) * lift[2] + (nb * oa + na * ob)
+
+    def wh_apply():
+        def apply(k, carry):
+            sw, sa, sb = carry
+            oa, ob = offu[0, inner], offu[1, inner]
+            a, b = jp[0, k, inner], jp[1, k, inner]
+            ja, jb = barj[0, k], barj[1, k]
+            sw = sw + (gs[k] * lift[0] + (b * oa - a * ob))
+            sa = sa + (lift[1] + oa * ja - ob * jb)
+            sb = sb + (lift[2] + oa * jb + ob * ja)
+            cw[k] += sw
+            ch[0, k] += sa
+            ch[1, k] += sb
+            up[0, k, inner] += oa
+            up[1, k, inner] += ob
+            return sw, sa, sb
+
+        lax.fori_loop(0, radii, apply, (zero,) * 3)
+
+    exchange(2, sum_h, part_h, tot_h, slot_h, pre_h, below_h, False, None, wh_apply)
+    for f in range(3):
+        cw[radii + f] = below_h[f * cols:(f + 1) * cols]
 
     for copy in (j_left, j_right, b_left, b_right, u_left, u_right):
         copy.wait_send()
@@ -376,8 +455,8 @@
     finish(2, sum_h, part_h, tot_h, slot_h, pre_h, False)
 
 
-def tail(step, bp, up, cw, ch, below_h, beta_out, u_out, w_out, h_out, wv, hv, sems):
-    radii, cols = cw.shape[0], cw.shape[1]
+def tail(step, bp, up, cw, ch, beta_out, u_out, w_out, h_out, wv, hv, sems):
+    radii, cols = ch.shape[1], ch.shape[2]
     rows = pl.ds(PAD, cols)
     copies = [pltpu.make_async_copy(bp.at[:, rows, :], beta_out, sems.at[0, 0])]
     copies += [pltpu.make_async_copy(up.at[f, :, rows, :], u_out.at[f], sems.at[1, f]) for f in range(2)]
@@ -387,9 +466,9 @@
     size = radii // parts
     for i in range(parts):
         def wh_final(k, c):
-            wv[k] = step * (cw[k] + below_h[:cols])
+            wv[k] = step * (cw[k] + cw[radii])
             for f in range(2):
-                hv[f, k] = step * (ch[f, k] + below_h[(f + 1) * cols:(f + 2) * cols])
+                hv[f, k] = step * (ch[f, k] + cw[radii + 1 + f])
             return c
 
         lax.fori_loop(i * size, (i + 1) * size, wh_final, 0, unroll=4)
@@ -418,12 +497,12 @@
             vm(2, radii, cols, lanes),
             vm(2, radii, lanes), vm(2, radii, lanes),
             vm(2, 2, radii, lanes), vm(2, 2, radii, lanes),
+            vm(radii, cols, lanes), vm(2, radii, cols, lanes), vm(radii, cols, lanes), vm(4, cols, lanes),
+            vm(tall, lanes), vm(cols, lanes), vm(2, cols, lanes), vm(2, tall, lanes), vm(3, cols, lanes),
         ]
         many = max(chips - 1, 1)
         for n in (1, 2, 3):
-            if n < 3:
-                scratch.append(vm(n * cols, lanes))
-            scratch += [vm(n * cols, lanes)] * 3 + [vm(many, n * cols, lanes), vm(n * cols, lanes)]
+            scratch += [vm(n * cols, lanes)] + [vm(n * cols, lanes)] * 3 + [vm(many, n * cols, lanes), vm(n * cols, lanes)]
         for n in (1, 2):
             scratch += [vm(2, n, lanes)] * 3 + [vm(many, 2, n, lanes)]
         dma = pltpu.SemaphoreType.DMA
@@ -435,19 +514,19 @@
         hbm = pl.BlockSpec(memory_space=pltpu.HBM)
         found = pl.pallas_call(
             functools.partial(kernel, shells, patches, step),
-            out_shape=(shape(radii, tall, lanes), shape(2, radii, tall, lanes), shape(radii, cols, lanes),
-                       shape(2, radii, cols, lanes), shape(3 * cols, lanes)),
+            out_shape=(shape(radii, tall, lanes), shape(2, radii, tall, lanes), shape(radii + 3, cols, lanes),
+                       shape(2, radii, cols, lanes)),
             in_specs=[hbm],
-            out_specs=(vmem,) * 5,
+            out_specs=(vmem,) * 4,
             scratch_shapes=scratch,
             compiler_params=pltpu.CompilerParams(
-                collective_id=0, has_side_effects=True, vmem_limit_bytes=24 * 1024 * 1024),
-        )(field_j)
+                collective_id=0, has_side_effects=True, vmem_limit_bytes=KERNEL_VMEM),
+        )(pltpu.with_memory_space_constraint(field_j, pltpu.HBM))
         return pl.pallas_call(
             functools.partial(tail, step),
             out_shape=(shape(radii, cols, lanes), shape(2, radii, cols, lanes), shape(radii, cols, lanes),
                        shape(2, radii, cols, lanes)),
-            in_specs=[vmem] * 5,
+            in_specs=[vmem] * 4,
             out_specs=(hbm,) * 4,
             scratch_shapes=[vm(radii, cols, lanes), vm(2, radii, cols, lanes), dma((4, 2))],
             compiler_params=pltpu.CompilerParams(vmem_limit_bytes=24 * 1024 * 1024),

time: 32.2 us -> 33.3 us (1.034)
  Pallas kernels: 30.2 us -> 32.5 us
  local copies, waits for them, and re-layouts: 1.22 us -> 0 us
    pallas_call x1, Pallas kernels: 28.4 us -> 30.8 us  [local(): pl.pallas_call(functools.partial(kernel, shells, patches, step), out_shap...]
    unnamed x2 -> x0, local copies, waits for them, and re-layouts: 1.22 us -> none
where the time goes in v3:
time: 33.3 us; the launch traced here: 33.2 us
  Pallas kernels  32.5 us (98%)
  between operations  0.64 us (2%)
    pallas_call x1, Pallas kernels, local(): pl.pallas_call(functools.partial(kernel, shells, patches, step), out_shap...  30.8 us
    pallas_call x1, Pallas kernels, local(): pl.pallas_call(functools.partial(tail, step), out_shape=(shape(radii, col...  1.73 us

profile of v3, /device:TPU:25, one launch (start us, length us, event | category | flops | bytes accessed | tf_op | source)
XLA Modules:
  0.0 33.2 jit_solution(2871333955236645222)
XLA Ops:
  0.6 30.8 %shard_map.46 = (f32[32,48,128]{2,1,0:T(8,128)S(1)}, f32[2,32,48,128]{3,2,1,0:T(8,128)S(1)}, f32[35,32,128]{2,1,0:T(8,128)S(1)}, f32[2,32,32,128]{3,2,1,0:T(8,128)S(1)}) custom-call(f32[2,32,32,128]{3,2,1,0:T(8,128)} %j_hbm.1), custom_call_target="tpu_custom_call" | custom-call | tf_op jit(solution)/shard_map/pallas_call | solution.py:515
  31.4 1.7 %shard_map.47 = (f32[32,32,128]{2,1,0:T(8,128)}, f32[2,32,32,128]{3,2,1,0:T(8,128)}, f32[32,32,128]{2,1,0:T(8,128)}, f32[2,32,32,128]{3,2,1,0:T(8,128)}) custom-call(f32[32,48,128]{2,1,0:T(8,128)S(1)} %get-tuple-element.8.bp, f32[2,32,48,128]{3,2,1,0:T(8,128)S(1)} %get-tuple-element.9.up, f32[35,32,128]{2,1,0:T(8,128)S(1)} %get-tuple-element.10.cw, ...), custom_call_target="tpu_custom_call" | custom-call | tf_op jit(solution)/shard_map/pallas_call | solution.py:525

commit v4 on v2

--- a/solution.py
+++ b/solution.py
@@ -23,7 +23,7 @@
 
 
 def kernel(shells, patches, step, j_hbm, bp, up, cw, ch, below_h,
-           jp, jnext, jedge, jhalo, barj, bedge, bhalo, uedge, uhalo,
+           jp, jnext, jedge, jhalo, barj, bedge, bhalo, uedge, uhalo, gs,
            below_b, sum_b, part_b, tot_b, slot_b, pre_b,
            below_u, sum_u, part_u, tot_u, slot_u, pre_u,
            sum_h, part_h, tot_h, slot_h, pre_h,
@@ -309,6 +309,7 @@
         sa, sb = carry
         beta = bp[k, inner]
         growth = jnp.exp(2.0 * beta)
+        gs[k] = growth
         br = theta(beta)
         bi = 0.5 * (bp[k, above] - bp[k, below])
         a, b = jp[0, k, inner], jp[1, k, inner]
@@ -343,7 +344,7 @@
     def wh_step(k, carry):
         sw, sa, sb = carry
         beta = bp[k, inner]
-        growth = jnp.exp(2.0 * beta)
+        growth = gs[k]
         a, b = jp[0, k, inner], jp[1, k, inner]
         ua, ub = up[0, k, inner], up[1, k, inner]
         ta, tb = theta(ua), theta(ub)
@@ -358,7 +359,7 @@
         ch[1, k] = sb
         return sw, sa, sb
 
-    sw, sa, sb = lax.fori_loop(0, radii, wh_step, (zero, zero, zero), unroll=2)
+    sw, sa, sb = lax.fori_loop(0, radii, wh_step, (zero, zero, zero))
     sum_h[:cols] = sw
     sum_h[cols:2 * cols] = sa
     sum_h[2 * cols:] = sb
@@ -417,7 +418,7 @@
             vm(2, radii, tall, lanes), vm(2, cols, lanes), vm(2, 2, radii, lanes), vm(2, 2, radii, lanes),
             vm(2, radii, cols, lanes),
             vm(2, radii, lanes), vm(2, radii, lanes),
-            vm(2, 2, radii, lanes), vm(2, 2, radii, lanes),
+            vm(2, 2, radii, lanes), vm(2, 2, radii, lanes), vm(radii, cols, lanes),
         ]
         many = max(chips - 1, 1)
         for n in (1, 2, 3):
@@ -442,7 +443,7 @@
             scratch_shapes=scratch,
             compiler_params=pltpu.CompilerParams(
                 collective_id=0, has_side_effects=True, vmem_limit_bytes=24 * 1024 * 1024),
-        )(field_j)
+        )(pltpu.with_memory_space_constraint(field_j, pltpu.HBM))
         return pl.pallas_call(
             functools.partial(tail, step),
             out_shape=(shape(radii, cols, lanes), shape(2, radii, cols, lanes), shape(radii, cols, lanes),

time: 32.2 us -> 32.1 us (level)
  local copies, waits for them, and re-layouts: 1.22 us -> 0 us
  Pallas kernels: 30.2 us -> 31.3 us
    unnamed x2 -> x0, local copies, waits for them, and re-layouts: 1.22 us -> none
    pallas_call x1, Pallas kernels: 28.4 us -> 29.6 us  [local(): pl.pallas_call(functools.partial(kernel, shells, patches, step), out_shap...]
where the time goes in v4:
time: 32.1 us; the launch traced here: 32 us
  Pallas kernels  31.3 us (98%)
  between operations  0.64 us (2%)
    pallas_call x1, Pallas kernels, local(): pl.pallas_call(functools.partial(kernel, shells, patches, step), out_shap...  29.6 us
    pallas_call x1, Pallas kernels, local(): pl.pallas_call(functools.partial(tail, step), out_shape=(shape(radii, col...  1.73 us

profile of v4, /device:TPU:25, one launch (start us, length us, event | category | flops | bytes accessed | tf_op | source)
XLA Modules:
  0.0 32.0 jit_solution(6186015774632515795)
XLA Ops:
  0.6 29.6 %shard_map.46 = (f32[32,48,128]{2,1,0:T(8,128)S(1)}, f32[2,32,48,128]{3,2,1,0:T(8,128)S(1)}, f32[32,32,128]{2,1,0:T(8,128)S(1)}, f32[2,32,32,128]{3,2,1,0:T(8,128)S(1)}, f32[96,128]{1,0:T(8,128)S(1)}) custom-call(f32[2,32,32,128]{3,2,1,0:T(8,128)} %j_hbm.1), custom_call_target="tpu_custom_call" | custom-call | tf_op jit(solution)/shard_map/pallas_call | solution.py:437
  30.2 1.7 %shard_map.47 = (f32[32,32,128]{2,1,0:T(8,128)}, f32[2,32,32,128]{3,2,1,0:T(8,128)}, f32[32,32,128]{2,1,0:T(8,128)}, f32[2,32,32,128]{3,2,1,0:T(8,128)}) custom-call(f32[32,48,128]{2,1,0:T(8,128)S(1)} %get-tuple-element.9.bp, f32[2,32,48,128]{3,2,1,0:T(8,128)S(1)} %get-tuple-element.10.up, f32[32,32,128]{2,1,0:T(8,128)S(1)} %get-tuple-element.11.cw, ...), custom_call_target="tpu_custom_call" | custom-call | tf_op jit(solution)/shard_map/pallas_call | solution.py:447

commit v5 on v4

--- a/solution.py
+++ b/solution.py
@@ -42,8 +42,11 @@
     below = slice(PAD - 1, PAD + cols - 1)
     before, after = slice(PAD - 1, PAD), slice(PAD + cols, PAD + cols + 1)
 
-    load = pltpu.make_async_copy(j_hbm, jp.at[:, :, pl.ds(PAD, cols), :], load_sem)
-    load.start()
+    loads = [
+        pltpu.make_async_copy(j_hbm.at[:, :, pl.ds(lo, n), :], jp.at[:, :, pl.ds(PAD + lo, n), :], load_sem.at[i])
+        for i, (lo, n) in enumerate(((0, 8), (cols - 8, 8), (8, cols - 16)))]
+    for load in loads:
+        load.start()
     barrier = pltpu.get_barrier_semaphore()
     for d in range(shells):
         there = lax.rem(shell + d, shells)
@@ -209,7 +212,8 @@
                 remote(pre.at[mine], pre.at[mine], fwd_sem.at[stage, 0], fwd_sem.at[stage, 1],
                        partner, patch).wait_send()
 
-    load.wait()
+    loads[0].wait()
+    loads[1].wait()
 
     def pack(k, c):
         for f in range(2):
@@ -227,6 +231,8 @@
     @pl.when(shell > 0)
     def _():
         remote(j_hbm.at[:, 0], jnext, rad_sem.at[0], rad_sem.at[1], shell - 1, patch).start()
+
+    loads[2].wait()
 
     def beta_step(k, next_of, spans, totals):
         new = []
@@ -328,7 +334,7 @@
     u_left.start()
     u_right.start()
     rims_u = (rim_u, rtot_u, rpart_u, rslot_u)
-    exchange(1, sum_u, part_u, tot_u, slot_u, pre_u, below_u, False, rims_u)
+    exchange(1, sum_u, part_u, tot_u, slot_u, pre_u, below_u, True, rims_u)
     u_left.wait_recv()
     u_right.wait_recv()
 
@@ -373,7 +379,7 @@
         remote(j_hbm.at[:, 0], jnext, rad_sem.at[0], rad_sem.at[1], shell - 1, patch).wait_send()
 
     finish(0, sum_b, part_b, tot_b, slot_b, pre_b, True, rims_b)
-    finish(1, sum_u, part_u, tot_u, slot_u, pre_u, False, rims_u)
+    finish(1, sum_u, part_u, tot_u, slot_u, pre_u, True, rims_u)
     finish(2, sum_h, part_h, tot_h, slot_h, pre_h, False)
 
 
@@ -428,7 +434,7 @@
         for n in (1, 2):
             scratch += [vm(2, n, lanes)] * 3 + [vm(many, 2, n, lanes)]
         dma = pltpu.SemaphoreType.DMA
-        scratch += [dma, dma((2,)), dma((3, 2)), dma((3, 2)), dma((3, 2)),
+        scratch += [dma((3,)), dma((2,)), dma((3, 2)), dma((3, 2)), dma((3, 2)),
                     dma((3, many, 2)), dma((3, many, 2)), dma((3, 2)),
                     dma((2, 2)), dma((2, 2)), dma((2, many, 2)), dma((2, many, 2))]
         shape = lambda *s: jax.ShapeDtypeStruct(s, f32)

time: 32.1 us -> 32.3 us (level)
  no operation moved by 1% of the time
where the time goes in v5:
time: 32.3 us; the launch traced here: 32.1 us
  Pallas kernels  31.5 us (98%)
  between operations  0.64 us (2%)
    pallas_call x1, Pallas kernels, local(): pl.pallas_call(functools.partial(kernel, shells, patches, step), out_shap...  29.8 us
    pallas_call x1, Pallas kernels, local(): pl.pallas_call(functools.partial(tail, step), out_shape=(shape(radii, col...  1.73 us

profile of v5, /device:TPU:25, one launch (start us, length us, event | category | flops | bytes accessed | tf_op | source)
XLA Modules:
  0.0 32.1 jit_solution(6513347135756708586)
XLA Ops:
  0.6 29.8 %shard_map.46 = (f32[32,48,128]{2,1,0:T(8,128)S(1)}, f32[2,32,48,128]{3,2,1,0:T(8,128)S(1)}, f32[32,32,128]{2,1,0:T(8,128)S(1)}, f32[2,32,32,128]{3,2,1,0:T(8,128)S(1)}, f32[96,128]{1,0:T(8,128)S(1)}) custom-call(f32[2,32,32,128]{3,2,1,0:T(8,128)} %j_hbm.1), custom_call_target="tpu_custom_call" | custom-call | tf_op jit(solution)/shard_map/pallas_call | solution.py:443
  30.4 1.7 %shard_map.47 = (f32[32,32,128]{2,1,0:T(8,128)}, f32[2,32,32,128]{3,2,1,0:T(8,128)}, f32[32,32,128]{2,1,0:T(8,128)}, f32[2,32,32,128]{3,2,1,0:T(8,128)}) custom-call(f32[32,48,128]{2,1,0:T(8,128)S(1)} %get-tuple-element.9.bp, f32[2,32,48,128]{3,2,1,0:T(8,128)S(1)} %get-tuple-element.10.up, f32[32,32,128]{2,1,0:T(8,128)S(1)} %get-tuple-element.11.cw, ...), custom_call_target="tpu_custom_call" | custom-call | tf_op jit(solution)/shard_map/pallas_call | solution.py:453

commit v6 on v5

--- a/solution.py
+++ b/solution.py
@@ -334,7 +334,7 @@
     u_left.start()
     u_right.start()
     rims_u = (rim_u, rtot_u, rpart_u, rslot_u)
-    exchange(1, sum_u, part_u, tot_u, slot_u, pre_u, below_u, True, rims_u)
+    exchange(1, sum_u, part_u, tot_u, slot_u, pre_u, below_u, False, rims_u)
     u_left.wait_recv()
     u_right.wait_recv()
 
@@ -379,7 +379,7 @@
         remote(j_hbm.at[:, 0], jnext, rad_sem.at[0], rad_sem.at[1], shell - 1, patch).wait_send()
 
     finish(0, sum_b, part_b, tot_b, slot_b, pre_b, True, rims_b)
-    finish(1, sum_u, part_u, tot_u, slot_u, pre_u, True, rims_u)
+    finish(1, sum_u, part_u, tot_u, slot_u, pre_u, False, rims_u)
     finish(2, sum_h, part_h, tot_h, slot_h, pre_h, False)
 
 

time: 32.3 us -> 32.1 us (level)
  no operation moved by 1% of the time
where the time goes in v6:
time: 32.1 us; the launch traced here: 32 us
  Pallas kernels  31.3 us (98%)
  between operations  0.64 us (2%)
    pallas_call x1, Pallas kernels, local(): pl.pallas_call(functools.partial(kernel, shells, patches, step), out_shap...  29.6 us
    pallas_call x1, Pallas kernels, local(): pl.pallas_call(functools.partial(tail, step), out_shape=(shape(radii, col...  1.73 us

profile of v6, /device:TPU:25, one launch (start us, length us, event | category | flops | bytes accessed | tf_op | source)
XLA Modules:
  0.0 32.0 jit_solution(5863096631181688257)
XLA Ops:
  0.6 29.6 %shard_map.46 = (f32[32,48,128]{2,1,0:T(8,128)S(1)}, f32[2,32,48,128]{3,2,1,0:T(8,128)S(1)}, f32[32,32,128]{2,1,0:T(8,128)S(1)}, f32[2,32,32,128]{3,2,1,0:T(8,128)S(1)}, f32[96,128]{1,0:T(8,128)S(1)}) custom-call(f32[2,32,32,128]{3,2,1,0:T(8,128)} %j_hbm.1), custom_call_target="tpu_custom_call" | custom-call | tf_op jit(solution)/shard_map/pallas_call | solution.py:443
  30.2 1.7 %shard_map.47 = (f32[32,32,128]{2,1,0:T(8,128)}, f32[2,32,32,128]{3,2,1,0:T(8,128)}, f32[32,32,128]{2,1,0:T(8,128)}, f32[2,32,32,128]{3,2,1,0:T(8,128)}) custom-call(f32[32,48,128]{2,1,0:T(8,128)S(1)} %get-tuple-element.9.bp, f32[2,32,48,128]{3,2,1,0:T(8,128)S(1)} %get-tuple-element.10.up, f32[32,32,128]{2,1,0:T(8,128)S(1)} %get-tuple-element.11.cw, ...), custom_call_target="tpu_custom_call" | custom-call | tf_op jit(solution)/shard_map/pallas_call | solution.py:453
